TPU v7x, 32 devices: a whole 2x2x4 slice. The times are simulated.
32 devices in a mesh: dp: 8 (over z, x), tp: 4 (over y, core).
Axes of the slice: x: 2, y: 2, z: 4, core: 2. Of those that a mesh axis runs over, the one named last changes fastest.
Arguments:
- activations: bfloat16 [2048, 4096], P('dp'), may hold values from -6 to 6
- out_grads: bfloat16 [2048, 4096], P('dp', 'tp'), may hold values from -6 to 6
- residual: bfloat16 [32768, 4096], P('dp', 'tp'), may hold values from -24 to 24
- right_prev: bfloat16 [4096, 32], P('tp'), may hold values from -6 to 6
Outputs:
- update: bfloat16 [4096, 4096], P(None, 'tp')
- left_basis: float32 [4096, 32], replicated
- right_factor: float32 [4096, 32], P('tp')
All inputs are finite; a program needn't handle non-finite values.
Results may differ from a plain program's by a relative error of at most 0.0061.
Values sent between devices are 32-bit elements; how exact they have to be, the bound alone decides.
A program may use at most 64 MiB of HBM per device.

v0:
```python
import jax
import jax.numpy as jnp
from jax import lax
from jax.sharding import PartitionSpec as P


def shards(activations, out_grads, residual, right_prev):
    product = lax.dot_general(
        activations, out_grads, (((0,), (0,)), ((), ())), preferred_element_type=jnp.float32
    )
    merged = (product + residual.astype(jnp.float32)).astype(jnp.bfloat16)
    shard_sum = lax.psum_scatter(
        jnp.dot(merged, right_prev, preferred_element_type=jnp.float32),
        "tp",
        scatter_dimension=0,
        tiled=True,
    )
    block_sum = lax.psum(shard_sum, "dp")
    block_gram = jnp.dot(block_sum.T, block_sum, precision=lax.Precision.HIGHEST)
    gram_matrix = lax.psum(block_gram, "tp")
    lower_factor = jnp.linalg.cholesky(gram_matrix)
    basis_block = lax.linalg.triangular_solve(
        lower_factor, block_sum, left_side=False, lower=True, transpose_a=True
    )
    left_basis = lax.all_gather(basis_block, "tp", axis=0, tiled=True)
    left_half = left_basis.astype(jnp.bfloat16)
    coeff_terms = lax.dot_general(
        merged, left_half, (((0,), (0,)), ((), ())), preferred_element_type=jnp.float32
    )
    right_factor = lax.psum(coeff_terms, "dp") / lax.axis_size("dp")
    update = jnp.dot(left_basis, right_factor.T, precision=lax.Precision.HIGHEST).astype(
        jnp.bfloat16
    )
    return (update, left_basis, right_factor)


def solution(mesh):
    in_specs = (P("dp", None), P("dp", "tp"), P("dp", "tp"), P("tp", None))
    out_specs = (P(None, "tp"), P(), P("tp", None))
    return jax.shard_map(shards, mesh=mesh, in_specs=in_specs, out_specs=out_specs, check_vma=False)
```

profile of v0, /device:TPU:0, one launch (start us, length us, event | category | flops | bytes accessed | tf_op | source)
XLA Modules:
  0.0 244.7 jit_solution(3257671253548092697)
XLA Ops:
  7.2 0.0 copy-start
  7.2 0.0 copy-start.3
  7.2 0.0 reduce-scatter.2.cloned.1.call-start
  7.2 1.5 copy-done
  8.8 6.0 %add_convert_fusion = bf16[4096,1024]{1,0:T(8,128)(2,1)S(1)} fusion(bf16[4096,1024]{1,0:T(8,128)(2,1)} %param.6, bf16[256,4096]{1,0:T(8,128)(2,1)S(1)} %copy-done, bf16[256,1024]{1,0:T(8,128)(2,1)} %param.5), kind=kOutput, calls=%fused_computation | convolution fusion | flops 2160066560 | bytes 19398656 | tf_op jit(solution)/shard_map/dot_general | solution.py:8
  14.7 0.0 copy-start.1
  14.7 3.4 %copy-done.1 = bf16[4096,1024]{1,0:T(8,128)(2,1)} copy-done((bf16[4096,1024]{1,0:T(8,128)(2,1)}, bf16[4096,1024]{1,0:T(8,128)(2,1)S(1)}, u32[]{:S(2)}) %copy-start.1) | copy-done | bytes 8388632
  18.1 0.0 copy-done.3
  18.1 3.4 %fusion.6 = f32[4096,32]{0,1:T(8,128)} fusion(bf16[4096,1024]{1,0:T(8,128)(2,1)S(1)} %add_convert_fusion, bf16[1024,32]{0,1:T(8,128)(2,1)S(1)} %copy-done.3), kind=kOutput, calls=%fused_computation.15 | convolution fusion | flops 268435456 | bytes 8978432 | tf_op jit(solution)/shard_map/dot_general | solution.py:13
  21.5 0.0 reduce-scatter.2.cloned.1.call-update
  21.5 0.0 all-reduce.3.cloned.1.call-start
  21.6 24.5 %reduce-scatter.2.cloned.1.call-done = f32[1024,32]{0,1:T(8,128)} async-done(((f32[4096,32]{0,1:T(8,128)}), f32[1024,32]{0,1:T(8,128)}) %reduce-scatter.2.cloned.1.call-update) | async-done | bytes 131088 | tf_op jit(solution)/shard_map/reduce_scatter | solution.py:12
  46.0 0.0 all-reduce.3.cloned.1.call-update
  46.1 0.0 all-reduce.5.cloned.1.call-start
  46.1 73.8 %all-reduce.3.cloned.1.call-done = f32[1024,32]{0,1:T(8,128)} async-done(((f32[1024,32]{0,1:T(8,128)}), f32[1024,32]{0,1:T(8,128)}) %all-reduce.3.cloned.1.call-update) | async-done | bytes 131088 | tf_op jit(solution)/shard_map/psum | solution.py:18
  119.9 1.2 fusion.7
  121.1 10.1 %psum.22 = f32[32,32]{0,1:T(8,128)S(1)} all-reduce(f32[32,32]{0,1:T(8,128)S(1)} %fusion.7), channel_id=1, replica_groups=mesh['dp'=8,'tp'=4] {'tp'}, use_global_device_ids=true, to_apply=%region_2.0 | all-reduce | flops 1024 | bytes 8192 | tf_op jit(solution)/shard_map/psum | solution.py:20
  131.3 0.1 copy.8
  131.3 2.9 %cholesky.16 = f32[32,32]{1,0:T(8,128)S(1)} custom-call(f32[32,32]{1,0:T(8,128)S(1)} %fusion.5), custom_call_target="Cholesky" | custom-call | tf_op jit(solution)/shard_map/jit(cholesky)/cholesky | solution.py:21
  134.3 0.6 compare_reduce_fusion
  134.9 0.7 fusion.2
  135.6 2.4 custom-call.6
  138.0 1.2 fusion.3
  139.3 7.3 %all_gather.3 = f32[4096,32]{0,1:T(8,128)S(1)} all-gather(f32[1024,32]{0,1:T(8,128)S(1)} %fusion.3), channel_id=1, replica_groups=mesh['dp'=8,'tp'=4] {'tp'}, dimensions={0}, use_global_device_ids=true | all-gather | bytes 655360 | tf_op jit(solution)/shard_map/all_gather | solution.py:25
  146.6 5.6 %fusion = f32[1024,32]{0,1:T(8,128)} fusion(bf16[4096,1024]{1,0:T(8,128)(2,1)} %copy-done.1, f32[4096,32]{0,1:T(8,128)S(1)} %all_gather.3), kind=kOutput, calls=%fused_computation.2 | convolution fusion | flops 268566528 | bytes 9043968 | tf_op jit(solution)/shard_map/dot_general | solution.py:27
  152.1 0.0 all-reduce.5.cloned.1.call-update
  152.2 69.1 %all-reduce.5.cloned.1.call-done = f32[1024,32]{0,1:T(8,128)} async-done(((f32[1024,32]{0,1:T(8,128)}), f32[1024,32]{0,1:T(8,128)}) %all-reduce.5.cloned.1.call-update) | async-done | bytes 131088 | tf_op jit(solution)/shard_map/psum | solution.py:30
  221.2 0.9 broadcast_multiply_fusion
  222.1 0.0 copy-start.2
  222.1 15.3 %convolution_convert_fusion = bf16[4096,1024]{1,0:T(8,128)(2,1)} fusion(f32[4096,32]{0,1:T(8,128)S(1)} %all_gather.3, f32[1024,32]{0,1:T(8,128)S(1)} %broadcast_multiply_fusion), kind=kOutput, calls=%fused_computation.1 | convolution fusion | flops 1614807040 | bytes 9043968 | tf_op jit(solution)/shard_map/dot_general | solution.py:31
  237.4 0.8 copy.13
  238.2 0.0 copy-done.2
  (2 shorter events, 0.0 us)
Async XLA Ops:
  7.2 1.6 copy-start
  7.2 10.9 %copy-start.3 = (bf16[1024,32]{0,1:T(8,128)(2,1)S(1)}, bf16[1024,32]{0,1:T(8,128)(2,1)}, u32[]{:S(2)}) copy-start(bf16[1024,32]{0,1:T(8,128)(2,1)} %param.7) | copy-start | bytes 196612
  7.2 38.8 %reduce-scatter.2.cloned.1.call-start = ((), (), s32[]{:S(2)}) async-start(), calls=%async_computation.1 | async-start | bytes 655360 | tf_op jit(solution)/shard_map/reduce_scatter | solution.py:12
  14.7 3.4 %copy-start.1 = (bf16[4096,1024]{1,0:T(8,128)(2,1)}, bf16[4096,1024]{1,0:T(8,128)(2,1)S(1)}, u32[]{:S(2)}) copy-start(bf16[4096,1024]{1,0:T(8,128)(2,1)S(1)} %add_convert_fusion) | copy-start | bytes 25165828
  21.5 98.4 %all-reduce.3.cloned.1.call-start = ((), (), s32[]{:S(2)}) async-start(), calls=%async_computation.2 | async-start | bytes 262144 | tf_op jit(solution)/shard_map/psum | solution.py:18
  46.1 175.2 %all-reduce.5.cloned.1.call-start = ((), (), s32[]{:S(2)}) async-start(), calls=%async_computation.3 | async-start | bytes 262144 | tf_op jit(solution)/shard_map/psum | solution.py:30
  222.1 16.1 %copy-start.2 = (f32[1024,32]{0,1:T(8,128)}, f32[1024,32]{0,1:T(8,128)S(1)}, u32[]{:S(2)}) copy-start(f32[1024,32]{0,1:T(8,128)S(1)} %broadcast_multiply_fusion) | copy-start | bytes 393220
Sparse Core Ops, SparseCore 0:
  21.6 24.3 reduce-scatter.1
  49.4 70.4 all-reduce.2
  152.3 68.8 all-reduce.4
where the time goes:
time: 245 us
  waiting for transfers between devices  167 us (68%)
  matrix products  32.6 us (13%)
  blocking collectives  17.4 us (7%)
  between operations  13.8 us (6%)
  other arithmetic  7.6 us (3%)
  local copies, waits for them, and re-layouts  5.8 us (2%)
    psum x1, waiting for transfers between devices, shards(): block_sum = lax.psum(shard_sum, 'dp')  73.8 us
    psum x1, waiting for transfers between devices, shards(): right_factor = lax.psum(coeff_terms, 'dp') / lax.axis_size('dp')  69.1 us
    reduce_scatter x1, waiting for transfers between devices, shards(): lax.psum_scatter(jnp.dot(merged, right_prev, preferred_element_type=jnp.f...  24.5 us
    dot_general x1, matrix products, shards(): jnp.dot(left_basis, right_factor.T, precision=lax.Precision.HIGHEST)  15.3 us
    psum x1, blocking collectives, shards(): gram_matrix = lax.psum(block_gram, 'tp')  10.1 us
    all_gather x1, blocking collectives, shards(): left_basis = lax.all_gather(basis_block, 'tp', axis=0, tiled=True)  7.28 us
    dot_general x1, matrix products, shards(): lax.dot_general(activations, out_grads, (((0,), (0,)), ((), ())), preferr...  5.95 us
    unnamed x9, local copies, waits for them, and re-layouts  5.73 us
  transfers between devices with their start and end apart: 3, of which 3 were waited for; matrix products, arithmetic and copies ran while one was open for 0% of the time, Pallas kernels for 0%

commit v1 on v0

--- a/solution.py
+++ b/solution.py
@@ -15,7 +15,11 @@
         scatter_dimension=0,
         tiled=True,
     )
-    block_sum = lax.psum(shard_sum, "dp")
+    block_sum = shard_sum
+    for hop in (1, 2, 4):
+        block_sum = block_sum + lax.ppermute(
+            block_sum, "dp", [(dev, dev ^ hop) for dev in range(8)]
+        )
     block_gram = jnp.dot(block_sum.T, block_sum, precision=lax.Precision.HIGHEST)
     gram_matrix = lax.psum(block_gram, "tp")
     lower_factor = jnp.linalg.cholesky(gram_matrix)

time: 245 us -> 190 us (0.78)
  waiting for transfers between devices: 167 us -> 108 us
  starting transfers between devices: 0.12 us -> 5.59 us
    psum x1 -> x0, waiting for transfers between devices: 73.8 us -> none  [shards(): block_sum = lax.psum(shard_sum, 'dp')]
    ppermute x0 -> x3, waiting for transfers between devices: none -> 12.1 us  [shards(): lax.ppermute(block_sum, 'dp', [(dev, dev ^ hop) for dev in range(8)])]
    ppermute x0 -> x3, starting transfers between devices: none -> 5.51 us  [shards(): lax.ppermute(block_sum, 'dp', [(dev, dev ^ hop) for dev in range(8)])]
  transfers between devices with their start and end apart: 3 -> 5, of which waited for: 3 -> 5; matrix products, arithmetic and copies ran while one was open for 0% -> 0% of each run, Pallas kernels for 0% -> 0%
where the time goes in v1:
time: 190 us; the launch traced here: 189 us
  waiting for transfers between devices  108 us (57%)
  matrix products  30.7 us (16%)
  blocking collectives  16.7 us (9%)
  between operations  14.1 us (7%)
  other arithmetic  8.56 us (5%)
  local copies, waits for them, and re-layouts  5.8 us (3%)
  starting transfers between devices  5.59 us (3%)
    psum x1, waiting for transfers between devices, shards(): right_factor = lax.psum(coeff_terms, 'dp') / lax.axis_size('dp')  71.3 us
    reduce_scatter x1, waiting for transfers between devices, shards(): lax.psum_scatter(jnp.dot(merged, right_prev, preferred_element_type=jnp.f...  24.5 us
    dot_general x1, matrix products, shards(): jnp.dot(left_basis, right_factor.T, precision=lax.Precision.HIGHEST)  15.3 us
    ppermute x3, waiting for transfers between devices, shards(): lax.ppermute(block_sum, 'dp', [(dev, dev ^ hop) for dev in range(8)])  12.1 us
    psum x1, blocking collectives, shards(): gram_matrix = lax.psum(block_gram, 'tp')  10.2 us
    all_gather x1, blocking collectives, shards(): left_basis = lax.all_gather(basis_block, 'tp', axis=0, tiled=True)  6.5 us
    dot_general x1, matrix products, shards(): lax.dot_general(activations, out_grads, (((0,), (0,)), ((), ())), preferr...  5.95 us
    unnamed x9, local copies, waits for them, and re-layouts  5.73 us
  transfers between devices with their start and end apart: 5, of which 5 were waited for; matrix products, arithmetic and copies ran while one was open for 0% of the time, Pallas kernels for 0%

profile of v1, /device:TPU:0, one launch (start us, length us, event | category | flops | bytes accessed | tf_op | source)
XLA Modules:
  0.0 189.5 jit_solution(7611215638912217870)
XLA Ops:
  7.2 0.0 copy-start
  7.2 0.0 reduce-scatter.2.cloned.1.call-start
  7.2 1.5 copy-done
  8.8 6.0 %add_convert_fusion = bf16[4096,1024]{1,0:T(8,128)(2,1)S(1)} fusion(bf16[4096,1024]{1,0:T(8,128)(2,1)} %param.6, bf16[256,4096]{1,0:T(8,128)(2,1)S(1)} %copy-done, bf16[256,1024]{1,0:T(8,128)(2,1)} %param.5), kind=kOutput, calls=%fused_computation | convolution fusion | flops 2160066560 | bytes 19398656 | tf_op jit(solution)/shard_map/dot_general | solution.py:8
  14.7 0.0 copy-start.1
  14.7 3.4 %copy-done.1 = bf16[4096,1024]{1,0:T(8,128)(2,1)} copy-done((bf16[4096,1024]{1,0:T(8,128)(2,1)}, bf16[4096,1024]{1,0:T(8,128)(2,1)S(1)}, u32[]{:S(2)}) %copy-start.1) | copy-done | bytes 8388632
  18.1 3.4 %fusion.6 = f32[4096,32]{0,1:T(8,128)} fusion(bf16[4096,1024]{1,0:T(8,128)(2,1)S(1)} %add_convert_fusion, bf16[1024,32]{0,1:T(8,128)(2,1)S(1)} %copy-done.3), kind=kOutput, calls=%fused_computation.15 | convolution fusion | flops 268435456 | bytes 8978432 | tf_op jit(solution)/shard_map/dot_general | solution.py:13
  21.5 0.0 reduce-scatter.2.cloned.1.call-update
  21.5 0.0 all-reduce.2.cloned.1.call-start
  21.6 24.5 %reduce-scatter.2.cloned.1.call-done = f32[1024,32]{0,1:T(8,128)} async-done(((f32[4096,32]{0,1:T(8,128)}), f32[1024,32]{0,1:T(8,128)}) %reduce-scatter.2.cloned.1.call-update) | async-done | bytes 131088 | tf_op jit(solution)/shard_map/reduce_scatter | solution.py:12
  46.0 1.5 collective-permute-start
  47.5 3.8 %collective-permute-done = f32[1024,32]{0,1:T(8,128)S(1)} collective-permute-done((f32[1024,32]{0,1:T(8,128)}, f32[1024,32]{0,1:T(8,128)S(1)}, u32[]{:S(2)}, u32[]{:S(2)}) %collective-permute-start) | collective-permute-done | bytes 131104 | tf_op jit(solution)/shard_map/ppermute | solution.py:20
  51.3 0.9 add.30
  52.2 1.6 collective-permute-start.1
  53.8 3.5 %collective-permute-done.1 = f32[1024,32]{0,1:T(8,128)S(1)} collective-permute-done((f32[1024,32]{0,1:T(8,128)S(1)}, f32[1024,32]{0,1:T(8,128)S(1)}, u32[]{:S(2)}, u32[]{:S(2)}) %collective-permute-start.1) | collective-permute-done | bytes 131104 | tf_op jit(solution)/shard_map/ppermute | solution.py:20
  57.3 2.5 %collective-permute-start.2 = (f32[1024,32]{0,1:T(8,128)S(1)}, f32[1024,32]{0,1:T(8,128)S(1)}, u32[]{:S(2)}, u32[]{:S(2)}) collective-permute-start(f32[1024,32]{0,1:T(8,128)S(1)} %add.31), channel_id=1, source_target_pairs={{0,16},{4,20},{8,24},{12,28},{16,0},{20,4},{24,8},{28,12},{1,17},{... | collective-permute-start | bytes 393224 | tf_op jit(solution)/shard_map/ppermute | solution.py:20
  59.8 4.8 %collective-permute-done.2 = f32[1024,32]{0,1:T(8,128)S(1)} collective-permute-done((f32[1024,32]{0,1:T(8,128)S(1)}, f32[1024,32]{0,1:T(8,128)S(1)}, u32[]{:S(2)}, u32[]{:S(2)}) %collective-permute-start.2) | collective-permute-done | bytes 131104 | tf_op jit(solution)/shard_map/ppermute | solution.py:20
  64.6 0.2 fusion.7
  64.9 10.2 %psum.14 = f32[32,32]{0,1:T(8,128)S(1)} all-reduce(f32[32,32]{0,1:T(8,128)S(1)} %fusion.7), channel_id=1, replica_groups=mesh['dp'=8,'tp'=4] {'tp'}, use_global_device_ids=true, to_apply=%region_1.0 | all-reduce | flops 1024 | bytes 8192 | tf_op jit(solution)/shard_map/psum | solution.py:24
  75.1 0.1 copy.8
  75.2 2.9 %cholesky.16 = f32[32,32]{1,0:T(8,128)S(1)} custom-call(f32[32,32]{1,0:T(8,128)S(1)} %fusion.5), custom_call_target="Cholesky" | custom-call | tf_op jit(solution)/shard_map/jit(cholesky)/cholesky | solution.py:25
  78.2 0.6 compare_reduce_fusion
  78.8 0.7 fusion.2
  79.5 2.4 %custom-call.6 = f32[1,32,32]{1,2,0:T(8,128)S(1)} custom-call(f32[1,32,32]{2,1,0:T(8,128)S(1)} %fusion.2), custom_call_target="InvertDiagBlocksLowerTriangular" | custom-call | tf_op jit(solution)/shard_map/triangular_solve | solution.py:26
  81.9 0.3 fusion.3
  82.2 6.5 %all_gather.3 = f32[4096,32]{0,1:T(8,128)S(1)} all-gather(f32[1024,32]{0,1:T(8,128)S(1)} %fusion.3), channel_id=1, replica_groups=mesh['dp'=8,'tp'=4] {'tp'}, dimensions={0}, use_global_device_ids=true | all-gather | bytes 655360 | tf_op jit(solution)/shard_map/all_gather | solution.py:29
  88.8 5.6 %fusion = f32[1024,32]{0,1:T(8,128)} fusion(bf16[4096,1024]{1,0:T(8,128)(2,1)} %copy-done.1, f32[4096,32]{0,1:T(8,128)S(1)} %all_gather.3), kind=kOutput, calls=%fused_computation.2 | convolution fusion | flops 268566528 | bytes 9043968 | tf_op jit(solution)/shard_map/dot_general | solution.py:31
  94.3 0.0 all-reduce.2.cloned.1.call-update
  94.4 71.3 %all-reduce.2.cloned.1.call-done = f32[1024,32]{0,1:T(8,128)} async-done(((f32[1024,32]{0,1:T(8,128)}), f32[1024,32]{0,1:T(8,128)}) %all-reduce.2.cloned.1.call-update) | async-done | bytes 131088 | tf_op jit(solution)/shard_map/psum | solution.py:34
  165.6 0.9 broadcast_multiply_fusion
  166.6 15.3 %convolution_convert_fusion = bf16[4096,1024]{1,0:T(8,128)(2,1)} fusion(f32[4096,32]{0,1:T(8,128)S(1)} %all_gather.3, f32[1024,32]{0,1:T(8,128)S(1)} %broadcast_multiply_fusion), kind=kOutput, calls=%fused_computation.1 | convolution fusion | flops 1614807040 | bytes 9043968 | tf_op jit(solution)/shard_map/dot_general | solution.py:35
  181.8 0.8 copy.12
  (8 shorter events, 0.1 us)
Async XLA Ops:
  7.2 1.6 copy-start
  7.2 10.9 %copy-start.3 = (bf16[1024,32]{0,1:T(8,128)(2,1)S(1)}, bf16[1024,32]{0,1:T(8,128)(2,1)}, u32[]{:S(2)}) copy-start(bf16[1024,32]{0,1:T(8,128)(2,1)} %param.7) | copy-start | bytes 196612
  7.2 38.8 %reduce-scatter.2.cloned.1.call-start = ((), (), s32[]{:S(2)}) async-start(), calls=%async_computation.1 | async-start | bytes 655360 | tf_op jit(solution)/shard_map/reduce_scatter | solution.py:12
  14.7 3.4 %copy-start.1 = (bf16[4096,1024]{1,0:T(8,128)(2,1)}, bf16[4096,1024]{1,0:T(8,128)(2,1)S(1)}, u32[]{:S(2)}) copy-start(bf16[4096,1024]{1,0:T(8,128)(2,1)S(1)} %add_convert_fusion) | copy-start | bytes 25165828
  21.5 144.1 %all-reduce.2.cloned.1.call-start = ((), (), s32[]{:S(2)}) async-start(), calls=%async_computation.2 | async-start | bytes 262144 | tf_op jit(solution)/shard_map/psum | solution.py:34
  46.0 5.3 %collective-permute-start = (f32[1024,32]{0,1:T(8,128)}, f32[1024,32]{0,1:T(8,128)S(1)}, u32[]{:S(2)}, u32[]{:S(2)}) collective-permute-start(f32[1024,32]{0,1:T(8,128)} %reduce-scatter.2.cloned.1.call-done), channel_id=1, source_target_pairs={{0,4},{4,0},{8,12},{12,8},{16,20},{20,16},{24,28},{28,24},{1,5},{5... | collective-permute-start | bytes 393224 | tf_op jit(solution)/shard_map/ppermute | solution.py:20
  52.2 5.0 %collective-permute-start.1 = (f32[1024,32]{0,1:T(8,128)S(1)}, f32[1024,32]{0,1:T(8,128)S(1)}, u32[]{:S(2)}, u32[]{:S(2)}) collective-permute-start(f32[1024,32]{0,1:T(8,128)S(1)} %add.30), channel_id=1, source_target_pairs={{0,8},{4,12},{8,0},{12,4},{16,24},{20,28},{24,16},{28,20},{1,9},{5... | collective-permute-start | bytes 393224 | tf_op jit(solution)/shard_map/ppermute | solution.py:20
  57.3 7.3 %collective-permute-start.2 = (f32[1024,32]{0,1:T(8,128)S(1)}, f32[1024,32]{0,1:T(8,128)S(1)}, u32[]{:S(2)}, u32[]{:S(2)}) collective-permute-start(f32[1024,32]{0,1:T(8,128)S(1)} %add.31), channel_id=1, source_target_pairs={{0,16},{4,20},{8,24},{12,28},{16,0},{20,4},{24,8},{28,12},{1,17},{... | collective-permute-start | bytes 393224 | tf_op jit(solution)/shard_map/ppermute | solution.py:20
  166.5 16.1 %copy-start.2 = (f32[1024,32]{0,1:T(8,128)}, f32[1024,32]{0,1:T(8,128)S(1)}, u32[]{:S(2)}) copy-start(f32[1024,32]{0,1:T(8,128)S(1)} %broadcast_multiply_fusion) | copy-start | bytes 393220
Sparse Core Ops, SparseCore 0:
  21.6 24.3 reduce-scatter.1
  94.5 71.1 all-reduce.1
